TPU v7x, 512 devices: a whole 4x4x16 slice. The times are simulated.
512 devices in a mesh: ctx: 64 (over z, y), dp: 8 (over x, core).
Axes of the slice: x: 4, y: 4, z: 16, core: 2. Of those that a mesh axis runs over, the one named last changes fastest.
Arguments:
- q_in: bfloat16 [8, 8192, 2048], P('dp', 'ctx'), may hold values from -6 to 6
- k_in: bfloat16 [8, 8192, 2048], P('dp', 'ctx'), may hold values from -6 to 6
- v_in: bfloat16 [8, 8192, 2048], P('dp', 'ctx'), may hold values from -6 to 6
- grad_out: bfloat16 [8, 8192, 2048], P('dp', 'ctx'), may hold values from -6 to 6
- short_filter: float32 [3, 3, 2048], replicated, may hold values from -3.5 to 3.5
- residue: float32 [2048, 8], replicated, may hold values from -2 to 2
- rate: float32 [8], replicated, may hold values from 0.00012207031 to 0.1
Outputs:
- mixed: bfloat16 [8, 8192, 2048], P('dp', 'ctx')
- grad_q: bfloat16 [8, 8192, 2048], P('dp', 'ctx')
- grad_k: bfloat16 [8, 8192, 2048], P('dp', 'ctx')
- grad_v: bfloat16 [8, 8192, 2048], P('dp', 'ctx')
- grad_residue: float32 [2048, 8], P('ctx')
- grad_short: float32 [3, 3, 2048], replicated
All inputs are finite; a program needn't handle non-finite values.
Results may differ from a plain program's by a relative error of at most 0.024.
Values may be sent and summed in bfloat16 or wider, within the bound.
A program may use at most 64 MiB of HBM per device.

v0:
```python
import jax
import jax.numpy as jnp
from jax import lax
from jax.sharding import PartitionSpec as P

BLOCK = 128
PRECISE = lax.Precision.HIGHEST


def passed_along(block, axis, distance):
    devices = range(lax.axis_size(axis))
    route = [(i - distance, i) for i in devices if i - distance in devices]
    return lax.ppermute(block, axis, route)


def mode_sweeps(source, cotangent, rates, columns, gains, front, behind):
    block_len = BLOCK
    block_count = source.shape[1]
    places = jnp.arange(block_len, dtype=jnp.float32)
    offset = places[:, None] - places[None, :]
    blocks = jnp.arange(block_count, dtype=jnp.float32)
    spacing = blocks[:, None] - blocks[None, :] - 1.0
    cot_f = cotangent.astype(jnp.float32)

    def one_mode(carry, item):
        conv_acc, back_acc = carry
        speed, column, start_fwd, start_back = item
        kernel = jnp.where(offset >= 0, jnp.exp(-speed * jnp.maximum(offset, 0.0)), 0.0).astype(
            jnp.bfloat16
        )
        passing = jnp.where(
            spacing >= 0, jnp.exp(-speed * block_len * jnp.maximum(spacing, 0.0)), 0.0
        )
        lead = jnp.exp(-speed * block_len * blocks)
        trail = jnp.exp(-speed * block_len * (block_count - 1.0 - blocks))
        scale_fwd = jnp.exp(-speed * (places + 1.0))
        scale_back = jnp.exp(-speed * (block_len - places))
        inside = jnp.einsum("ts,cns->cnt", kernel, source, preferred_element_type=jnp.float32)
        entering = (
            jnp.einsum("nk,ck->cn", passing, inside[..., block_len - 1], precision=PRECISE)
            + lead[None, :] * start_fwd[:, None]
        )
        forward = inside + scale_fwd[None, None, :] * entering[..., None]
        conv_acc = conv_acc + column[:, None, None] * forward
        grad_row = jnp.sum(forward * cot_f, axis=(1, 2))
        inside_back = jnp.einsum(
            "ts,cnt->cns", kernel, cotangent, preferred_element_type=jnp.float32
        )
        entering_back = (
            jnp.einsum("kn,ck->cn", passing, inside_back[..., 0], precision=PRECISE)
            + trail[None, :] * start_back[:, None]
        )
        backward = inside_back + scale_back[None, None, :] * entering_back[..., None]
        back_acc = back_acc + column[:, None, None] * backward
        return ((conv_acc, back_acc), grad_row)

    zeros_acc = jnp.zeros(source.shape, jnp.float32)
    (conv_sum, back_sum), grads = lax.scan(
        one_mode, (zeros_acc, zeros_acc), (rates, columns, front, behind)
    )
    grads = gains[:, None] * grads
    return (conv_sum, back_sum, grads.T)


def shards(q_in, k_in, v_in, grad_out, short_filter, residue, rate):
    row_count = q_in.shape[1]
    width = q_in.shape[2]
    inputs = (q_in[0], k_in[0], v_in[0])
    tails = jnp.stack([item[row_count - 2 :] for item in inputs])
    before = passed_along(tails, "ctx", 1)
    extended = [
        jnp.concatenate([before[branch], inputs[branch]], axis=0).astype(jnp.float32)
        for branch in range(3)
    ]
    shorts = []
    for branch in range(3):
        total = short_filter[branch, 0][None, :] * extended[branch][2 : 2 + row_count]
        for tap_at in range(1, 3):
            total = (
                total
                + short_filter[branch, tap_at][None, :]
                * extended[branch][2 - tap_at : 2 - tap_at + row_count]
            )
        shorts.append(total)
    query, keyed, valued = shorts
    gated = (keyed * valued).astype(jnp.bfloat16)
    cot_out = grad_out[0].astype(jnp.float32)
    d_conv = (cot_out * query).astype(jnp.bfloat16)
    gains = jnp.sqrt(1.0 - jnp.exp(-2.0 * rate))
    weights = residue * gains[None, :]
    modes = rate.shape[0]
    ctx_count = lax.axis_size("ctx")
    channel_share = width // ctx_count
    owned, incoming = (
        lax.all_to_all(gated, "ctx", split_axis=1, concat_axis=0, tiled=True),
        lax.all_to_all(d_conv, "ctx", split_axis=1, concat_axis=0, tiled=True),
    )
    total_rows = owned.shape[0]
    block_count = total_rows // BLOCK
    owned_lanes = owned.T.reshape(channel_share, block_count, BLOCK)
    incoming_lanes = incoming.T.reshape(channel_share, block_count, BLOCK)
    columns = lax.dynamic_slice_in_dim(
        weights, lax.axis_index("ctx") * channel_share, channel_share, 0
    ).T
    zero_start = jnp.zeros((modes, channel_share), jnp.float32)
    conv_sum, back_sum, partial_value = mode_sweeps(
        owned_lanes, incoming_lanes, rate, columns, gains, zero_start, zero_start
    )
    conv_rows = conv_sum.reshape(channel_share, total_rows).T.astype(jnp.bfloat16)
    back_rows = back_sum.reshape(channel_share, total_rows).T.astype(jnp.bfloat16)
    conv, d_gated = (
        lax.all_to_all(conv_rows, "ctx", split_axis=0, concat_axis=1, tiled=True),
        lax.all_to_all(back_rows, "ctx", split_axis=0, concat_axis=1, tiled=True),
    )
    grad_residue = lax.psum(partial_value, "dp")
    conv_f = conv.astype(jnp.float32)
    mixed = (query * conv_f).astype(jnp.bfloat16)
    gated_back = d_gated.astype(jnp.float32)
    d_shorts = (cot_out * conv_f, gated_back * valued, gated_back * keyed)
    heads = jnp.stack([item[:2] for item in d_shorts])
    after = passed_along(heads.astype(jnp.bfloat16), "ctx", -1).astype(heads.dtype)
    grads = []
    partial_short = []
    for branch in range(3):
        ahead_rows = jnp.concatenate([d_shorts[branch], after[branch]], axis=0)
        total = short_filter[branch, 0][None, :] * ahead_rows[0:row_count]
        for tap_at in range(1, 3):
            total = (
                total
                + short_filter[branch, tap_at][None, :] * ahead_rows[tap_at : tap_at + row_count]
            )
        grads.append(total.astype(jnp.bfloat16)[None])
        partial_short.append(
            jnp.stack(
                [
                    jnp.sum(
                        d_shorts[branch] * extended[branch][2 - tap_at : 2 - tap_at + row_count],
                        axis=0,
                    )
                    for tap_at in range(3)
                ]
            )
        )
    grad_short = lax.psum(jnp.stack(partial_short), ("ctx", "dp"))
    return (mixed[None], grads[0], grads[1], grads[2], grad_residue, grad_short)


def solution(mesh):
    placed = (
        P("dp", "ctx", None),
        P("dp", "ctx", None),
        P("dp", "ctx", None),
        P("dp", "ctx", None),
        P(),
        P(),
        P(),
    )
    return jax.shard_map(
        shards,
        mesh=mesh,
        in_specs=placed,
        out_specs=(
            P("dp", "ctx", None),
            P("dp", "ctx", None),
            P("dp", "ctx", None),
            P("dp", "ctx", None),
            P("ctx", None),
            P(),
        ),
        check_vma=False,
    )
```

profile of v0, /device:TPU:1, one launch (start us, length us, event | category | flops | bytes accessed | tf_op | source)
XLA Modules:
  0.0 703.1 jit_solution(16576350189797462453)
XLA Ops:
  7.2 0.8 slice.139
  7.9 0.8 slice.140
  8.7 0.8 slice.141
  9.5 4.0 collective-permute-start
  13.6 1.0 fusion.78
  14.6 1.3 copy.33
  15.9 1.3 copy.31
  17.9 0.8 maximum_convert_fusion.1
  18.7 4.5 multiply_convert_fusion
  23.2 18.3 %all-to-all-start = ((bf16[128,64,32]{0,2,1:T(8,128)(2,1)}), bf16[128,64,32]{0,2,1:T(8,128)(2,1)S(1)}, u32[]{:S(2)}, u32[]{:S(2)}) async-start(bf16[128,64,32]{0,2,1:T(8,128)(2,1)} %bitcast.16), calls=%async_computation | async-start | bytes 1048576 | tf_op jit(solution)/shard_map/all_to_all | solution.py:95
  42.9 1.3 copy-done.4
  44.2 2.4 fusion.51
  46.6 24.2 %all-to-all-done = bf16[128,64,32]{0,2,1:T(8,128)(2,1)S(1)} async-done(((bf16[128,64,32]{0,2,1:T(8,128)(2,1)}), bf16[128,64,32]{0,2,1:T(8,128)(2,1)S(1)}, u32[]{:S(2)}, u32[]{:S(2)}) %all-to-all-start) | async-done | bytes 524320 | tf_op jit(solution)/shard_map/all_to_all | solution.py:95
  70.7 8.6 %all-to-all-start.1 = ((bf16[128,64,32]{0,2,1:T(8,128)(2,1)}), bf16[128,64,32]{0,2,1:T(8,128)(2,1)S(1)}, u32[]{:S(2)}, u32[]{:S(2)}) async-start(bf16[128,64,32]{0,2,1:T(8,128)(2,1)} %bitcast.20), calls=%async_computation.1 | async-start | bytes 1048576 | tf_op jit(solution)/shard_map/all_to_all | solution.py:96
  79.4 0.8 fusion.77
  80.3 0.9 copy.54
  81.2 27.1 %all-to-all-done.1 = bf16[128,64,32]{0,2,1:T(8,128)(2,1)S(1)} async-done(((bf16[128,64,32]{0,2,1:T(8,128)(2,1)}), bf16[128,64,32]{0,2,1:T(8,128)(2,1)S(1)}, u32[]{:S(2)}, u32[]{:S(2)}) %all-to-all-start.1) | async-done | bytes 524320 | tf_op jit(solution)/shard_map/all_to_all | solution.py:96
  108.4 0.9 copy.55
  109.3 1.1 bitcast_convert_fusion
  110.5 60.8 %while.16 = (s32[]{:T(128)}, f32[32,64,128]{2,1,0:T(8,128)}, f32[32,64,128]{2,1,0:T(8,128)}, f32[8,32]{1,0:T(8,128)S(1)}, f32[8,32]{1,0:T(8,128)S(1)}, /*index=5...) while((s32[]{:T(128)}, f32[32,64,128]{2,1,0:T(8,128)}, ...), condition=%wide.region_2.3_spmd.clone.clone, body=%wide.region_0.2_spmd.clone.clone.sunk | while | flops 140759840 | bytes 12668891 | solution.py:58
  111.8 1.4 convolution_bitcast_fusion.5
  114.9 2.2 multiply_reduce_fusion.11
  118.4 1.4 convolution_bitcast_fusion.5
  121.5 3.3 multiply_reduce_fusion.11
  126.1 1.4 convolution_bitcast_fusion.5
  129.2 3.3 multiply_reduce_fusion.11
  133.8 1.4 convolution_bitcast_fusion.5
  137.0 3.3 multiply_reduce_fusion.11
  141.6 1.4 convolution_bitcast_fusion.5
  144.7 3.3 multiply_reduce_fusion.11
  149.3 1.4 convolution_bitcast_fusion.5
  152.5 3.3 multiply_reduce_fusion.11
  157.1 1.4 convolution_bitcast_fusion.5
  160.2 3.3 multiply_reduce_fusion.11
  164.8 1.4 convolution_bitcast_fusion.5
  167.9 3.3 multiply_reduce_fusion.11
  171.3 1.4 convert_element_type.94
  172.7 1.1 copy_bitcast_fusion
  173.8 9.2 %all-to-all-start.3 = ((bf16[64,128,32]{1,2,0:T(8,128)(2,1)}), bf16[64,128,32]{1,2,0:T(8,128)(2,1)}, u32[]{:S(2)}, u32[]{:S(2)}) async-start(bf16[64,128,32]{1,2,0:T(8,128)(2,1)} %copy_bitcast_fusion), calls=%async_computation.3 | async-start | bytes 1048576 | tf_op jit(solution)/shard_map/all_to_all | solution.py:113
  183.1 1.1 copy_bitcast_fusion.1
  184.3 27.9 %all-to-all-done.3 = bf16[64,128,32]{1,2,0:T(8,128)(2,1)} async-done(((bf16[64,128,32]{1,2,0:T(8,128)(2,1)}), bf16[64,128,32]{1,2,0:T(8,128)(2,1)}, u32[]{:S(2)}, u32[]{:S(2)}) %all-to-all-start.3) | async-done | bytes 524320 | tf_op jit(solution)/shard_map/all_to_all | solution.py:113
  212.1 8.9 %all-to-all-start.2 = ((bf16[64,128,32]{1,2,0:T(8,128)(2,1)}), bf16[64,128,32]{1,2,0:T(8,128)(2,1)}, u32[]{:S(2)}, u32[]{:S(2)}) async-start(bf16[64,128,32]{1,2,0:T(8,128)(2,1)} %copy_bitcast_fusion.1), calls=%async_computation.2 | async-start | bytes 1048576 | tf_op jit(solution)/shard_map/all_to_all | solution.py:112
  221.2 14.6 %psum.14 = f32[32,8]{0,1:T(8,128)} all-reduce(f32[32,8]{0,1:T(8,128)S(1)} %multiply_bitcast_fusion), channel_id=1, replica_groups=mesh['ctx'=64,'dp'=8] {'dp'}, use_global_device_ids=true, to_apply=%region_3.4 | all-reduce | flops 256 | bytes 2048 | tf_op jit(solution)/shard_map/psum | solution.py:115
  235.8 6.3 multiply_reduce_fusion.6
  242.1 1.0 copy-done.7
  243.1 0.8 fusion.72
  243.9 1.2 copy.40
  245.2 0.9 fusion.73
  246.0 1.2 copy.41
  247.3 2.9 all-to-all-done.2
  250.2 3.0 multiply_reduce_fusion.9
  253.5 1.3 collective-permute-start.1
  255.6 1.0 copy.43
  256.6 1.5 collective-permute-done.1
  258.1 0.9 copy.42
  259.4 1.0 copy-done.10
  260.4 2.2 fusion.76
  262.6 2.2 fusion.75
  264.8 2.2 fusion.74
  266.9 1.0 copy.46
  268.0 1.0 copy.45
  269.0 1.0 copy.44
  270.0 424.7 %all-reduce.2.cloned.1.call-done = f32[3,3,2048]{2,1,0:T(4,128)} async-done(((f32[3,3,2048]{2,1,0:T(4,128)}), f32[3,3,2048]{2,1,0:T(4,128)}) %all-reduce.2.cloned.1.call-update) | async-done | bytes 73744 | tf_op jit(solution)/shard_map/psum | solution.py:144
  694.7 1.5 copy.80
  (151 shorter events, 22.3 us)
Async XLA Ops:
  9.5 7.7 %collective-permute-start = (bf16[3,2,2048]{2,1,0:T(2,128)(2,1)S(1)}, bf16[3,2,2048]{2,1,0:T(2,128)(2,1)S(1)}, u32[]{:S(2)}, u32[]{:S(2)}) collective-permute-start(bf16[3,2,2048]{2,1,0:T(2,128)(2,1)S(1)} %pad_maximum_fusion.4), channel_id=1, source_target_pairs={{0,8},{8,16},{16,24},{24,32},{32,40},{40,48},{48,56},{56,64},{64,7... | collective-permute-start | bytes 73736 | tf_op jit(solution)/shard_map/ppermute | solution.py:13
  18.7 4.5 copy-start.1
  18.7 4.5 copy-start.3
  18.7 22.8 %copy-start.13 = (bf16[1,128,2048]{2,1,0:T(8,128)(2,1)S(1)}, bf16[1,128,2048]{2,1,0:T(8,128)(2,1)}, u32[]{:S(2)}) copy-start(bf16[1,128,2048]{2,1,0:T(8,128)(2,1)} %param.9) | copy-start | bytes 1572868
  23.2 18.6 %copy-start.14 = (bf16[1,128,2048]{2,1,0:T(8,128)(2,1)S(1)}, bf16[1,128,2048]{2,1,0:T(8,128)(2,1)}, u32[]{:S(2)}) copy-start(bf16[1,128,2048]{2,1,0:T(8,128)(2,1)} %param.12) | copy-start | bytes 1572868
  23.2 47.5 %all-to-all-start = ((bf16[128,64,32]{0,2,1:T(8,128)(2,1)}), bf16[128,64,32]{0,2,1:T(8,128)(2,1)S(1)}, u32[]{:S(2)}, u32[]{:S(2)}) async-start(bf16[128,64,32]{0,2,1:T(8,128)(2,1)} %bitcast.16), calls=%async_computation | async-start | bytes 1048576 | tf_op jit(solution)/shard_map/all_to_all | solution.py:95
  42.1 4.5 copy-start.11
  42.8 1.4 copy-start.4
  44.2 35.2 %copy-start.15 = (f32[8]{0:T(128)S(1)}, f32[8]{0:T(128)}, u32[]{:S(2)}) copy-start(f32[8]{0:T(128)} %param.15) | copy-start | bytes 100
  70.7 37.6 %all-to-all-start.1 = ((bf16[128,64,32]{0,2,1:T(8,128)(2,1)}), bf16[128,64,32]{0,2,1:T(8,128)(2,1)S(1)}, u32[]{:S(2)}, u32[]{:S(2)}) async-start(bf16[128,64,32]{0,2,1:T(8,128)(2,1)} %bitcast.20), calls=%async_computation.1 | async-start | bytes 1048576 | tf_op jit(solution)/shard_map/all_to_all | solution.py:96
  111.7 2.0 copy-start.6
  118.3 2.0 copy-start.6
  126.1 2.0 copy-start.6
  133.8 2.0 copy-start.6
  141.6 2.0 copy-start.6
  149.3 2.0 copy-start.6
  157.0 2.0 copy-start.6
  164.8 2.0 copy-start.6
  171.3 11.8 %copy-start = (f32[32,64,128]{2,1,0:T(8,128)S(1)}, f32[32,64,128]{2,1,0:T(8,128)}, u32[]{:S(2)}) copy-start(f32[32,64,128]{2,1,0:T(8,128)} %get-tuple-element.87) | copy-start | bytes 3145732
  173.8 38.3 %all-to-all-start.3 = ((bf16[64,128,32]{1,2,0:T(8,128)(2,1)}), bf16[64,128,32]{1,2,0:T(8,128)(2,1)}, u32[]{:S(2)}, u32[]{:S(2)}) async-start(bf16[64,128,32]{1,2,0:T(8,128)(2,1)} %copy_bitcast_fusion), calls=%async_computation.3 | async-start | bytes 1048576 | tf_op jit(solution)/shard_map/all_to_all | solution.py:113
  183.0 52.7 %copy-start.2 = (f32[130,2048]{0,1:T(8,128)S(1)}, f32[130,2048]{0,1:T(8,128)}, u32[]{:S(2)}) copy-start(f32[130,2048]{0,1:T(8,128)} %copy-done.1) | copy-start | bytes 3194884
  212.1 38.0 %all-to-all-start.2 = ((bf16[64,128,32]{1,2,0:T(8,128)(2,1)}), bf16[64,128,32]{1,2,0:T(8,128)(2,1)}, u32[]{:S(2)}, u32[]{:S(2)}) async-start(bf16[64,128,32]{1,2,0:T(8,128)(2,1)} %copy_bitcast_fusion.1), calls=%async_computation.2 | async-start | bytes 1048576 | tf_op jit(solution)/shard_map/all_to_all | solution.py:112
  221.0 473.7 %all-reduce.2.cloned.1.call-start = ((), (), s32[]{:S(2)}) async-start(), calls=%async_computation.4 | async-start | bytes 196608 | tf_op jit(solution)/shard_map/psum | solution.py:144
  242.1 1.0 copy-start.7
  242.1 8.1 %copy-start.9 = (f32[128,2048]{0,1:T(8,128)}, f32[128,2048]{0,1:T(8,128)S(1)}, u32[]{:S(2)}) copy-start(f32[128,2048]{0,1:T(8,128)S(1)} %get-tuple-element.228) | copy-start | bytes 3145732
  242.1 8.0 %copy-start.5 = (f32[130,2048]{0,1:T(8,128)S(1)}, f32[130,2048]{0,1:T(8,128)}, u32[]{:S(2)}) copy-start(f32[130,2048]{0,1:T(8,128)} %copy-done.4) | copy-start | bytes 3194884
  253.2 2.4 copy-start.12
  253.5 4.6 collective-permute-start.1
  259.1 1.2 copy-start.10
  259.4 3.2 copy-start.8
Sparse Core Ops, SparseCore 0:
  255.7 438.9 all-reduce.1
where the time goes:
time: 705 us; the launch traced here: 703 us
  waiting for transfers between devices  508 us (72%)
  other arithmetic  54 us (8%)
  starting transfers between devices  50.4 us (7%)
  local copies, waits for them, and re-layouts  39.1 us (6%)
  matrix products  16.5 us (2%)
  blocking collectives  14.6 us (2%)
  between operations  14.5 us (2%)
    psum x1, waiting for transfers between devices, shards(): grad_short = lax.psum(jnp.stack(partial_short), ('ctx', 'dp'))  425 us
    all_to_all x1, waiting for transfers between devices, shards(): lax.all_to_all(back_rows, 'ctx', split_axis=0, concat_axis=1, tiled=True)  27.9 us
    all_to_all x1, waiting for transfers between devices, shards(): lax.all_to_all(d_conv, 'ctx', split_axis=1, concat_axis=0, tiled=True)  27.1 us
    reduce_sum x8, other arithmetic, one_mode(): grad_row = jnp.sum(forward * cot_f, axis=(1, 2))  25.3 us
    all_to_all x1, waiting for transfers between devices, shards(): lax.all_to_all(gated, 'ctx', split_axis=1, concat_axis=0, tiled=True)  24.2 us
    all_to_all x1, starting transfers between devices, shards(): lax.all_to_all(gated, 'ctx', split_axis=1, concat_axis=0, tiled=True)  18.3 us
    unnamed x46, local copies, waits for them, and re-layouts  15 us
    psum x1, blocking collectives, shards(): grad_residue = lax.psum(partial_value, 'dp')  14.6 us
  transfers between devices with their start and end apart: 7, of which 6 were waited for; matrix products, arithmetic and copies ran while one was open for 5% of the time, Pallas kernels for 0%

commit v1 on v0

--- a/solution.py
+++ b/solution.py
@@ -141,7 +141,9 @@
                 ]
             )
         )
-    grad_short = lax.psum(jnp.stack(partial_short), ("ctx", "dp"))
+    grad_short = jnp.stack(partial_short)
+    for mesh_axis in ("ctx", "dp"):
+        grad_short = lax.psum(grad_short, mesh_axis)
     return (mixed[None], grads[0], grads[1], grads[2], grad_residue, grad_short)
 
 

time: 705 us -> 592 us (0.84)
  waiting for transfers between devices: 508 us -> 394 us
    psum x1 -> x2, waiting for transfers between devices: 425 us -> 311 us  [shards(): grad_short = lax.psum(grad_short, mesh_axis)]
    unnamed x46 -> x52, local copies, waits for them, and re-layouts: 15 us -> 15.1 us
  transfers between devices with their start and end apart: 7 -> 8, of which waited for: 6 -> 7; matrix products, arithmetic and copies ran while one was open for 5% -> 6% of each run, Pallas kernels for 0% -> 0%
where the time goes in v1:
time: 592 us; the launch traced here: 591 us
  waiting for transfers between devices  394 us (67%)
  other arithmetic  55.6 us (9%)
  starting transfers between devices  50.5 us (9%)
  local copies, waits for them, and re-layouts  39.1 us (7%)
  matrix products  16.5 us (3%)
  blocking collectives  14.6 us (2%)
  between operations  14.5 us (2%)
    psum x2, waiting for transfers between devices, shards(): grad_short = lax.psum(grad_short, mesh_axis)  311 us
    all_to_all x1, waiting for transfers between devices, shards(): lax.all_to_all(back_rows, 'ctx', split_axis=0, concat_axis=1, tiled=True)  27.9 us
    all_to_all x1, waiting for transfers between devices, shards(): lax.all_to_all(d_conv, 'ctx', split_axis=1, concat_axis=0, tiled=True)  27.1 us
    reduce_sum x8, other arithmetic, one_mode(): grad_row = jnp.sum(forward * cot_f, axis=(1, 2))  25.3 us
    all_to_all x1, waiting for transfers between devices, shards(): lax.all_to_all(gated, 'ctx', split_axis=1, concat_axis=0, tiled=True)  24.2 us
    all_to_all x1, starting transfers between devices, shards(): lax.all_to_all(gated, 'ctx', split_axis=1, concat_axis=0, tiled=True)  18.3 us
    unnamed x52, local copies, waits for them, and re-layouts  15.1 us
    psum x1, blocking collectives, shards(): grad_residue = lax.psum(partial_value, 'dp')  14.6 us
  transfers between devices with their start and end apart: 8, of which 7 were waited for; matrix products, arithmetic and copies ran while one was open for 6% of the time, Pallas kernels for 0%

profile of v1, /device:TPU:1, one launch (start us, length us, event | category | flops | bytes accessed | tf_op | source)
XLA Modules:
  0.0 590.8 jit_solution(9653473878698204474)
XLA Ops:
  7.2 0.8 slice.139
  7.9 0.8 slice.140
  8.7 0.8 slice.141
  9.5 4.0 collective-permute-start
  13.6 1.0 fusion.78
  14.6 1.3 copy.33
  15.9 1.3 copy.31
  17.9 0.8 maximum_convert_fusion.1
  18.7 4.5 multiply_convert_fusion
  23.2 18.3 %all-to-all-start = ((bf16[128,64,32]{0,2,1:T(8,128)(2,1)}), bf16[128,64,32]{0,2,1:T(8,128)(2,1)S(1)}, u32[]{:S(2)}, u32[]{:S(2)}) async-start(bf16[128,64,32]{0,2,1:T(8,128)(2,1)} %bitcast.16), calls=%async_computation | async-start | bytes 1048576 | tf_op jit(solution)/shard_map/all_to_all | solution.py:95
  42.9 1.3 copy-done.4
  44.2 2.4 fusion.51
  46.6 24.2 %all-to-all-done = bf16[128,64,32]{0,2,1:T(8,128)(2,1)S(1)} async-done(((bf16[128,64,32]{0,2,1:T(8,128)(2,1)}), bf16[128,64,32]{0,2,1:T(8,128)(2,1)S(1)}, u32[]{:S(2)}, u32[]{:S(2)}) %all-to-all-start) | async-done | bytes 524320 | tf_op jit(solution)/shard_map/all_to_all | solution.py:95
  70.7 8.6 %all-to-all-start.1 = ((bf16[128,64,32]{0,2,1:T(8,128)(2,1)}), bf16[128,64,32]{0,2,1:T(8,128)(2,1)S(1)}, u32[]{:S(2)}, u32[]{:S(2)}) async-start(bf16[128,64,32]{0,2,1:T(8,128)(2,1)} %bitcast.20), calls=%async_computation.1 | async-start | bytes 1048576 | tf_op jit(solution)/shard_map/all_to_all | solution.py:96
  80.3 0.9 copy.54
  81.2 27.1 %all-to-all-done.1 = bf16[128,64,32]{0,2,1:T(8,128)(2,1)S(1)} async-done(((bf16[128,64,32]{0,2,1:T(8,128)(2,1)}), bf16[128,64,32]{0,2,1:T(8,128)(2,1)S(1)}, u32[]{:S(2)}, u32[]{:S(2)}) %all-to-all-start.1) | async-done | bytes 524320 | tf_op jit(solution)/shard_map/all_to_all | solution.py:96
  108.4 0.9 copy.55
  109.3 1.1 bitcast_convert_fusion
  110.5 60.8 %while.16 = (s32[]{:T(128)}, f32[32,64,128]{2,1,0:T(8,128)}, f32[32,64,128]{2,1,0:T(8,128)}, f32[8,32]{1,0:T(8,128)S(1)}, f32[8,32]{1,0:T(8,128)S(1)}, /*index=5...) while((s32[]{:T(128)}, f32[32,64,128]{2,1,0:T(8,128)}, ...), condition=%wide.region_2.3_spmd.clone.clone, body=%wide.region_0.2_spmd.clone.clone.sunk | while | flops 140759840 | bytes 12668891 | solution.py:58
  111.8 1.4 convolution_bitcast_fusion.5
  114.9 2.2 multiply_reduce_fusion.11
  118.4 1.4 convolution_bitcast_fusion.5
  121.5 3.3 multiply_reduce_fusion.11
  126.1 1.4 convolution_bitcast_fusion.5
  129.2 3.3 multiply_reduce_fusion.11
  133.8 1.4 convolution_bitcast_fusion.5
  137.0 3.3 multiply_reduce_fusion.11
  141.6 1.4 convolution_bitcast_fusion.5
  144.7 3.3 multiply_reduce_fusion.11
  149.3 1.4 convolution_bitcast_fusion.5
  152.4 3.3 multiply_reduce_fusion.11
  157.1 1.4 convolution_bitcast_fusion.5
  160.2 3.3 multiply_reduce_fusion.11
  164.8 1.4 convolution_bitcast_fusion.5
  167.9 3.3 multiply_reduce_fusion.11
  171.3 1.4 convert_element_type.94
  172.7 1.1 copy_bitcast_fusion
  173.8 9.2 %all-to-all-start.3 = ((bf16[64,128,32]{1,2,0:T(8,128)(2,1)}), bf16[64,128,32]{1,2,0:T(8,128)(2,1)}, u32[]{:S(2)}, u32[]{:S(2)}) async-start(bf16[64,128,32]{1,2,0:T(8,128)(2,1)} %copy_bitcast_fusion), calls=%async_computation.3 | async-start | bytes 1048576 | tf_op jit(solution)/shard_map/all_to_all | solution.py:113
  183.1 1.1 copy_bitcast_fusion.1
  184.3 27.9 %all-to-all-done.3 = bf16[64,128,32]{1,2,0:T(8,128)(2,1)} async-done(((bf16[64,128,32]{1,2,0:T(8,128)(2,1)}), bf16[64,128,32]{1,2,0:T(8,128)(2,1)}, u32[]{:S(2)}, u32[]{:S(2)}) %all-to-all-start.3) | async-done | bytes 524320 | tf_op jit(solution)/shard_map/all_to_all | solution.py:113
  212.1 8.9 %all-to-all-start.2 = ((bf16[64,128,32]{1,2,0:T(8,128)(2,1)}), bf16[64,128,32]{1,2,0:T(8,128)(2,1)}, u32[]{:S(2)}, u32[]{:S(2)}) async-start(bf16[64,128,32]{1,2,0:T(8,128)(2,1)} %copy_bitcast_fusion.1), calls=%async_computation.2 | async-start | bytes 1048576 | tf_op jit(solution)/shard_map/all_to_all | solution.py:112
  221.2 14.6 %psum.21 = f32[32,8]{0,1:T(8,128)} all-reduce(f32[32,8]{0,1:T(8,128)S(1)} %multiply_bitcast_fusion), channel_id=1, replica_groups=mesh['ctx'=64,'dp'=8] {'dp'}, use_global_device_ids=true, to_apply=%region_3.4 | all-reduce | flops 256 | bytes 2048 | tf_op jit(solution)/shard_map/psum | solution.py:115
  235.8 6.2 %multiply_reduce_fusion.6 = (f32[2048]{0:T(1024)S(1)}, f32[2048]{0:T(1024)S(1)}, f32[2048]{0:T(1024)S(1)}, f32[128,2048]{0,1:T(8,128)S(1)}, f32[2048]{0:T(1024)S...) fusion(f32[130,2048]{0,1:T(8,128)S(1)} %copy-done.2, f32[128,2048]{0,1:T(8,128)} %get-tuple-element.211, ...), kind=kLoop, calls=%fused_computation.106 | loop fusion | flops 3919872 | bytes 11059200 | tf_op jit(solution)/shard_map/reduce_sum | solution.py:136
  242.0 1.0 copy-done.7
  243.0 0.8 fusion.72
  243.9 1.2 copy.40
  245.1 0.9 fusion.73
  246.0 1.2 copy.41
  247.2 2.9 all-to-all-done.2
  250.1 3.0 multiply_reduce_fusion.9
  253.5 1.3 collective-permute-start.1
  255.6 1.0 copy.43
  256.6 1.4 collective-permute-done.1
  258.1 0.9 copy.42
  259.4 1.0 copy-done.10
  260.4 2.7 fusion.76
  263.1 2.8 fusion.75
  265.9 237.1 %all-reduce.3.cloned.1.call-done = f32[3,3,2048]{2,1,0:T(4,128)} async-done(((f32[3,3,2048]{2,1,0:T(4,128)}), f32[3,3,2048]{2,1,0:T(4,128)}) %all-reduce.3.cloned.1.call-update) | async-done | bytes 73744 | tf_op jit(solution)/shard_map/psum | solution.py:146
  503.0 2.8 fusion.74
  505.8 1.0 copy.46
  506.8 1.0 copy.45
  507.8 1.0 copy.44
  508.8 73.6 %all-reduce.5.cloned.1.call-done = f32[3,3,2048]{2,1,0:T(4,128)} async-done(((f32[3,3,2048]{2,1,0:T(4,128)}), f32[3,3,2048]{2,1,0:T(4,128)}) %all-reduce.5.cloned.1.call-update) | async-done | bytes 73744 | tf_op jit(solution)/shard_map/psum | solution.py:146
  582.4 1.5 copy.81
  (160 shorter events, 23.1 us)
Async XLA Ops:
  9.5 7.7 %collective-permute-start = (bf16[3,2,2048]{2,1,0:T(2,128)(2,1)S(1)}, bf16[3,2,2048]{2,1,0:T(2,128)(2,1)S(1)}, u32[]{:S(2)}, u32[]{:S(2)}) collective-permute-start(bf16[3,2,2048]{2,1,0:T(2,128)(2,1)S(1)} %pad_maximum_fusion.4), channel_id=1, source_target_pairs={{0,8},{8,16},{16,24},{24,32},{32,40},{40,48},{48,56},{56,64},{64,7... | collective-permute-start | bytes 73736 | tf_op jit(solution)/shard_map/ppermute | solution.py:13
  18.7 4.5 copy-start.1
  18.7 4.5 copy-start.3
  18.7 22.8 %copy-start.16 = (bf16[1,128,2048]{2,1,0:T(8,128)(2,1)S(1)}, bf16[1,128,2048]{2,1,0:T(8,128)(2,1)}, u32[]{:S(2)}) copy-start(bf16[1,128,2048]{2,1,0:T(8,128)(2,1)} %param.9) | copy-start | bytes 1572868
  23.2 18.6 %copy-start.17 = (bf16[1,128,2048]{2,1,0:T(8,128)(2,1)S(1)}, bf16[1,128,2048]{2,1,0:T(8,128)(2,1)}, u32[]{:S(2)}) copy-start(bf16[1,128,2048]{2,1,0:T(8,128)(2,1)} %param.12) | copy-start | bytes 1572868
  23.2 47.5 %all-to-all-start = ((bf16[128,64,32]{0,2,1:T(8,128)(2,1)}), bf16[128,64,32]{0,2,1:T(8,128)(2,1)S(1)}, u32[]{:S(2)}, u32[]{:S(2)}) async-start(bf16[128,64,32]{0,2,1:T(8,128)(2,1)} %bitcast.16), calls=%async_computation | async-start | bytes 1048576 | tf_op jit(solution)/shard_map/all_to_all | solution.py:95
  42.1 4.5 copy-start.11
  42.9 1.3 copy-start.4
  44.2 35.2 %copy-start.18 = (f32[8]{0:T(128)S(1)}, f32[8]{0:T(128)}, u32[]{:S(2)}) copy-start(f32[8]{0:T(128)} %param.15) | copy-start | bytes 100
  70.7 37.6 %all-to-all-start.1 = ((bf16[128,64,32]{0,2,1:T(8,128)(2,1)}), bf16[128,64,32]{0,2,1:T(8,128)(2,1)S(1)}, u32[]{:S(2)}, u32[]{:S(2)}) async-start(bf16[128,64,32]{0,2,1:T(8,128)(2,1)} %bitcast.20), calls=%async_computation.1 | async-start | bytes 1048576 | tf_op jit(solution)/shard_map/all_to_all | solution.py:96
  111.7 2.0 copy-start.6
  118.3 2.0 copy-start.6
  126.1 2.0 copy-start.6
  133.8 2.0 copy-start.6
  141.5 2.0 copy-start.6
  149.3 2.0 copy-start.6
  157.0 2.0 copy-start.6
  164.8 2.0 copy-start.6
  171.3 11.8 %copy-start = (f32[32,64,128]{2,1,0:T(8,128)S(1)}, f32[32,64,128]{2,1,0:T(8,128)}, u32[]{:S(2)}) copy-start(f32[32,64,128]{2,1,0:T(8,128)} %get-tuple-element.87) | copy-start | bytes 3145732
  173.8 38.3 %all-to-all-start.3 = ((bf16[64,128,32]{1,2,0:T(8,128)(2,1)}), bf16[64,128,32]{1,2,0:T(8,128)(2,1)}, u32[]{:S(2)}, u32[]{:S(2)}) async-start(bf16[64,128,32]{1,2,0:T(8,128)(2,1)} %copy_bitcast_fusion), calls=%async_computation.3 | async-start | bytes 1048576 | tf_op jit(solution)/shard_map/all_to_all | solution.py:113
  183.0 52.7 %copy-start.2 = (f32[130,2048]{0,1:T(8,128)S(1)}, f32[130,2048]{0,1:T(8,128)}, u32[]{:S(2)}) copy-start(f32[130,2048]{0,1:T(8,128)} %copy-done.1) | copy-start | bytes 3194884
  212.1 38.0 %all-to-all-start.2 = ((bf16[64,128,32]{1,2,0:T(8,128)(2,1)}), bf16[64,128,32]{1,2,0:T(8,128)(2,1)}, u32[]{:S(2)}, u32[]{:S(2)}) async-start(bf16[64,128,32]{1,2,0:T(8,128)(2,1)} %copy_bitcast_fusion.1), calls=%async_computation.2 | async-start | bytes 1048576 | tf_op jit(solution)/shard_map/all_to_all | solution.py:112
  221.0 281.9 %all-reduce.3.cloned.1.call-start = ((), (), s32[]{:S(2)}) async-start(), calls=%async_computation.4 | async-start | bytes 196608 | tf_op jit(solution)/shard_map/psum | solution.py:146
  242.0 1.0 copy-start.7
  242.0 8.1 %copy-start.9 = (f32[128,2048]{0,1:T(8,128)}, f32[128,2048]{0,1:T(8,128)S(1)}, u32[]{:S(2)}) copy-start(f32[128,2048]{0,1:T(8,128)S(1)} %get-tuple-element.228) | copy-start | bytes 3145732
  242.0 8.1 %copy-start.5 = (f32[130,2048]{0,1:T(8,128)S(1)}, f32[130,2048]{0,1:T(8,128)}, u32[]{:S(2)}) copy-start(f32[130,2048]{0,1:T(8,128)} %copy-done.4) | copy-start | bytes 3194884
  253.1 2.5 copy-start.15
  253.5 4.6 collective-permute-start.1
  255.6 326.8 %all-reduce.5.cloned.1.call-start = ((), (), s32[]{:S(2)}) async-start(), calls=%async_computation.5 | async-start | bytes 196608 | tf_op jit(solution)/shard_map/psum | solution.py:146
  259.1 1.2 copy-start.10
  259.4 3.8 copy-start.8
  265.9 239.9 %copy-start.12 = (bf16[1,128,2048]{1,2,0:T(8,128)(2,1)S(1)}, bf16[1,128,2048]{1,2,0:T(8,128)(2,1)}, u32[]{:S(2)}) copy-start(bf16[1,128,2048]{1,2,0:T(8,128)(2,1)} %fusion.76) | copy-start | bytes 1572868
  265.9 240.9 %copy-start.13 = (bf16[1,128,2048]{1,2,0:T(8,128)(2,1)S(1)}, bf16[1,128,2048]{1,2,0:T(8,128)(2,1)}, u32[]{:S(2)}) copy-start(bf16[1,128,2048]{1,2,0:T(8,128)(2,1)} %fusion.75) | copy-start | bytes 1572868
  505.8 2.0 copy-start.14
Sparse Core Ops, SparseCore 0:
  255.7 247.2 all-reduce.2
  505.3 77.0 all-reduce.4
